TPU v7x, 32 devices: a whole 2x2x4 slice. The times are simulated.
32 devices in a mesh: grp: 4 (over y, x), seq: 8 (over z, core).
Axes of the slice: x: 2, y: 2, z: 4, core: 2. Of those that a mesh axis runs over, the one named last changes fastest.
Arguments:
- queries: bfloat16 [1024, 64, 192], P('seq', 'grp'), may hold values from -6 to 6
- key_cache: bfloat16 [4, 8192, 192], P('grp', 'seq'), may hold values from -6 to 6
- group_value_cache: bfloat16 [4, 8192, 128], P('grp', 'seq'), may hold values from -6 to 6
- coarse_keys: bfloat16 [4, 512, 192], P('grp', 'seq'), may hold values from -6 to 6
- coarse_values: bfloat16 [4, 512, 128], P('grp', 'seq'), may hold values from -6 to 6
- hidden: bfloat16 [1024, 2560], P('seq'), may hold values from -6 to 6
- gate_weight: bfloat16 [4, 2560, 32], P('grp'), may hold values from -0.125 to 0.125
- out_weight: bfloat16 [8192, 2560], P('grp'), may hold values from -0.09375 to 0.09375
- selected: int32 [4, 8, 16], P('grp', 'seq'), may hold values from 0 to 127, as said below
Outputs:
- layer_out: bfloat16 [1024, 2560], P('seq', 'grp')
Inputs may be any that keep to these rules, and one draw needn't show every extreme that they name: selected[g, t] lists 16 distinct blocks of 64 positions for tile t of group g; the first is block 0; none starts after the tile's last query position; at most 4 of them lie within one index of seq's 1024 positions.
All inputs are finite; a program needn't handle non-finite values.
Results may differ from a plain program's by a relative error of at most 0.013.
Values may be sent and summed in bfloat16 or wider, within the bound.
A program may use at most 128 MiB of HBM per device.

v0:
```python
import math
import jax
import jax.numpy as jnp
from jax import lax
from jax.sharding import PartitionSpec as P

BLK = 64
SEL = 16
TILE = 128
CSTRIDE = 16
CLEN = 32
NEGATIVE = -1e30


def online_block(folded, part_keys, part_values, query_rows, row_pos, key_pos, score_scale):
    running, row_total, summed_out = folded
    logit_scores = (
        lax.dot_general(
            query_rows, part_keys, (((1,), (1,)), ((), ())), preferred_element_type=jnp.float32
        )
        * score_scale
    )
    logit_scores = jnp.where(key_pos[None, :] <= row_pos[:, None], logit_scores, -jnp.inf)
    new_max = jnp.maximum(running, jnp.max(logit_scores, axis=1))
    factor = jnp.exp(running - new_max)
    weights = jnp.exp(logit_scores - new_max[:, None])
    row_total = row_total * factor + jnp.sum(weights, axis=1)
    summed_out = summed_out * factor[:, None] + jnp.dot(
        weights.astype(jnp.bfloat16), part_values, preferred_element_type=jnp.float32
    )
    return (new_max, row_total, summed_out)


def shards(
    queries,
    key_cache,
    group_value_cache,
    coarse_keys,
    coarse_values,
    hidden,
    gate_weight,
    out_weight,
    selected,
):
    seq_count = lax.axis_size("seq")
    seq_index = lax.axis_index("seq")
    ctx_dev = key_cache.shape[1]
    context = ctx_dev * seq_count
    heads_here = queries.shape[1]
    key_width = queries.shape[2]
    value_width = group_value_cache.shape[2]
    score_scale = key_width ** (-0.5)
    query_rows = queries.reshape(TILE * heads_here, key_width)
    query_pos = context - TILE * seq_count + seq_index * TILE + jnp.arange(TILE, dtype=jnp.int32)
    row_pos = jnp.repeat(query_pos, heads_here)
    row_count = TILE * heads_here
    fold_start = (
        jnp.full((row_count,), NEGATIVE, jnp.float32),
        jnp.zeros((row_count,), jnp.float32),
        jnp.zeros((row_count, value_width), jnp.float32),
    )
    requests = lax.all_gather(selected[0], "seq", axis=0, tiled=True)
    blocks_dev = ctx_dev // BLK
    slot_cap = max(1, 2 * SEL // seq_count)
    owners = requests // blocks_dev
    earlier = jnp.tril(jnp.ones((SEL, SEL), jnp.int32), -1)
    same_owner = (owners[:, :, None] == owners[:, None, :]).astype(jnp.int32)
    order_rank = jnp.sum(same_owner * earlier[None], axis=2)
    served = owners == seq_index
    slot_ids = jnp.arange(slot_cap, dtype=jnp.int32)
    matches = (served[:, :, None] & (order_rank[:, :, None] == slot_ids[None, None, :])).astype(
        jnp.int32
    )
    local_block = jnp.sum(matches * (requests - seq_index * blocks_dev)[:, :, None], axis=1)
    filled = jnp.sum(matches, axis=1) > 0
    block_keys_grouped = key_cache[0].reshape(blocks_dev, BLK, key_width)
    value_blocks = group_value_cache[0].reshape(blocks_dev, BLK, value_width)
    outgoing = jnp.concatenate(
        [
            jnp.take(block_keys_grouped, local_block, axis=0),
            jnp.take(value_blocks, local_block, axis=0),
        ],
        axis=3,
    )
    outgoing = jnp.where(filled[:, :, None, None], outgoing, jnp.zeros_like(outgoing))
    incoming = lax.all_to_all(outgoing, "seq", split_axis=0, concat_axis=0, tiled=True)
    piece_keys = lax.all_gather(coarse_keys[0], "seq", axis=0, tiled=True)
    piece_values = lax.all_gather(coarse_values[0], "seq", axis=0, tiled=True)
    length = piece_keys.shape[0]
    span_rows = math.gcd(length, 512)

    def advance(loop_index, state_now):
        offset = loop_index * span_rows
        part_keys = lax.dynamic_slice_in_dim(piece_keys, offset, span_rows, 0)
        part_values = lax.dynamic_slice_in_dim(piece_values, offset, span_rows, 0)
        key_pos = (offset + jnp.arange(span_rows, dtype=jnp.int32)) * CSTRIDE + CLEN - 1
        return online_block(
            state_now, part_keys, part_values, query_rows, row_pos, key_pos, score_scale
        )

    coarse_state = lax.fori_loop(0, length // span_rows, advance, fold_start)
    coarse_out = coarse_state[2] / coarse_state[1][:, None]
    own_list = selected[0, 0]
    own_owner = own_list // blocks_dev
    own_rank = jnp.sum(
        (own_owner[:, None] == own_owner[None, :]).astype(jnp.int32) * earlier, axis=1
    )
    picked_rows = incoming[own_owner, own_rank].reshape(SEL * BLK, key_width + value_width)
    picked_keys = picked_rows[:, :key_width]
    picked_values = picked_rows[:, key_width:]
    picked_pos = (own_list[:, None] * BLK + jnp.arange(BLK, dtype=jnp.int32)[None, :]).reshape(-1)
    picked_state = online_block(
        fold_start, picked_keys, picked_values, query_rows, row_pos, picked_pos, score_scale
    )
    picked_out = picked_state[2] / picked_state[1][:, None]
    gate_logits = jnp.dot(hidden, gate_weight[0], preferred_element_type=jnp.float32)
    gate_coarse = jax.nn.sigmoid(gate_logits[:, :heads_here])
    gate_picked = jax.nn.sigmoid(gate_logits[:, heads_here:])
    mixed_heads = gate_coarse[:, :, None] * coarse_out.reshape(
        TILE, heads_here, value_width
    ) + gate_picked[:, :, None] * picked_out.reshape(TILE, heads_here, value_width)
    attended = mixed_heads.astype(jnp.bfloat16).reshape(TILE, heads_here * value_width)
    partial_value = jnp.dot(attended, out_weight, preferred_element_type=jnp.float32)
    result = lax.psum_scatter(
        partial_value.astype(jnp.bfloat16), "grp", scatter_dimension=1, tiled=True
    )
    return result


def solution(mesh):
    return jax.shard_map(
        shards,
        mesh=mesh,
        in_specs=(
            P("seq", "grp", None),
            P("grp", "seq", None),
            P("grp", "seq", None),
            P("grp", "seq", None),
            P("grp", "seq", None),
            P("seq", None),
            P("grp", None, None),
            P("grp", None),
            P("grp", "seq", None),
        ),
        out_specs=P("seq", "grp"),
        check_vma=False,
    )
```

profile of v0, /device:TPU:0, one launch (start us, length us, event | category | flops | bytes accessed | tf_op | source)
XLA Modules:
  0.0 154.2 jit_solution(9140498446499711631)
XLA Ops:
  6.5 13.7 %all-gather.2 = s32[8,1,16]{2,1,0:T(1,128)S(1)} all-gather(s32[1,1,16]{2,1,0:T(1,128)} %param.17), channel_id=4, replica_groups=mesh['grp'=4,'seq'=8] {'seq'}, dimensions={0}, use_global_device_ids=true | all-gather | bytes 576 | tf_op jit(solution)/shard_map/all_gather | solution.py:62
  20.3 0.7 bitcast_multiply_fusion.2
  22.0 1.2 copy.40
  23.2 0.6 gather_fusion
  23.8 1.6 %gather_fusion.1 = bf16[32,64,128]{2,1,0:T(8,128)(2,1)S(1)} fusion(bf16[16,64,128]{2,1,0:T(8,128)(2,1)} %bitcast.90, s32[1024]{0:T(1024)S(1)} %pad_clamp_fusion), kind=kCustom, calls=%fused_computation.1 | custom fusion | bytes 1048704 | tf_op jit(solution)/shard_map/jit(_take)/gather | solution.py:81
  25.8 1.9 %maximum_select_fusion = bf16[8,4,64,320]{3,2,1,0:T(8,128)(2,1)} fusion(bf16[8,4,64,128]{3,2,1,0:T(8,128)(2,1)S(1)} %broadcast_select_fusion.1, bf16[8,4,64,192]{3,2,1,0:T(8,128)(2,1)S(1)} %broadcast_select_fusion, pred[8,4]{1,0:T(8,128)(4,1)S(1)} %copy.38), kind=kLoop, calls=%fused_computation.20 | loop fusion | flops 3276800 | bytes 2621472 | tf_op jit(solution)/shard_map/jit(_where)/select_n | solution.py:85
  27.7 3.6 %all-to-all-start = ((bf16[8,4,64,320]{3,2,1,0:T(8,128)(2,1)}), bf16[8,4,64,320]{3,2,1,0:T(8,128)(2,1)S(1)}, u32[]{:S(2)}, u32[]{:S(2)}) async-start(bf16[8,4,64,320]{3,2,1,0:T(8,128)(2,1)} %maximum_select_fusion), calls=%async_computation | async-start | bytes 3145728 | tf_op jit(solution)/shard_map/all_to_all | solution.py:86
  31.5 45.0 %all-gather.1 = bf16[1,512,128]{2,1,0:T(8,128)(2,1)} all-gather(bf16[1,64,128]{2,1,0:T(8,128)(2,1)S(1)} %copy-done.5), channel_id=3, replica_groups=mesh['grp'=4,'seq'=8] {'seq'}, dimensions={1}, use_global_device_ids=true | all-gather | bytes 147456 | tf_op jit(solution)/shard_map/all_gather | solution.py:88
  76.7 1.8 %copy.36 = bf16[128,16,192]{2,1,0:T(8,128)(2,1)S(1)} copy(bf16[128,16,192]{0,2,1:T(8,128)(2,1)} %param.9) | data formatting | bytes 1572864 | tf_op args[0]
  78.6 14.4 %all-gather = bf16[1,512,192]{2,1,0:T(8,128)(2,1)S(1)} all-gather(bf16[1,64,192]{2,1,0:T(8,128)(2,1)S(1)} %copy-done.4), channel_id=2, replica_groups=mesh['grp'=4,'seq'=8] {'seq'}, dimensions={1}, use_global_device_ids=true | all-gather | bytes 221184 | tf_op jit(solution)/shard_map/all_gather | solution.py:87
  92.9 0.8 fusion.47
  93.8 0.6 fusion.6
  94.6 2.1 %fusion.8 = f32[2048,128]{1,0:T(8,128)} fusion(f32[2048,512]{0,1:T(8,128)S(1)} %get-tuple-element.49, f32[2048]{0:T(1024)S(1)} %broadcast_maximum_fusion.1, f32[2048]{0:T(1024)S(1)} %get-tuple-element.38, f32[2048]{0:T(1024)S(1)} %get-tuple-element.36, bf16[1,512,128]{2,1,0:T(8,128)(2,1)S(1)} %copy-done.3), kind=kOutput, calls=%fused_computation.16 | convolution fusion | flops 271056896 | bytes 5398528 | tf_op jit(solution)/shard_map/while/body/eval_jaxpr/dot_general | solution.py:28
  96.7 1.4 reshape.242
  98.7 1.5 %gather_fusion.2 = bf16[16,64,320]{2,1,0:T(8,128)(2,1)} fusion(bf16[8,4,64,320]{3,2,1,0:T(8,128)(2,1)S(1)} %all-to-all-done, s32[16]{0:T(128)S(1)} %fusion.42), kind=kCustom, calls=%fused_computation.2 | custom fusion | bytes 1310848 | tf_op jit(solution)/shard_map/gather | solution.py:108
  100.2 2.7 %fusion.2 = (f32[2048]{0:T(1024)S(1)}, f32[1024,2048]{1,0:T(8,128)S(1)}) fusion(s32[2048]{0:T(1024)S(1)} %le.51, s32[1024]{0:T(1024)S(1)} %add.162, bf16[2048,192]{1,0:T(8,128)(2,1)} %bitcast.89, bf16[1024,320]{1,0:T(8,128)(2,1)} %bitcast.91), kind=kOutput, calls=%fused_computation.7 | convolution fusion | flops 813692928 | bytes 9981952 | tf_op jit(solution)/shard_map/dot_general | solution.py:18
  103.0 2.4 %fusion = f32[2048]{0:T(1024)S(1)} fusion(f32[1024,2048]{1,0:T(8,128)S(1)} %get-tuple-element.47, f32[2048]{0:T(1024)S(1)} %broadcast_maximum_fusion, s32[2048]{0:T(1024)S(1)} %le.51, s32[1024]{0:T(1024)S(1)} %add.162), kind=kLoop, calls=%fused_computation.5 | loop fusion | flops 10483712 | bytes 8417280 | tf_op jit(solution)/shard_map/reduce_sum | solution.py:27
  105.4 4.6 %fusion.14 = f32[2048,128]{1,0:T(8,128)} fusion(f32[1024,2048]{1,0:T(8,128)S(1)} %get-tuple-element.47, f32[2048]{0:T(1024)S(1)} %broadcast_maximum_fusion, s32[2048]{0:T(1024)S(1)} %le.51, s32[1024]{0:T(1024)S(1)} %add.162, f32[2048]{0:T(1024)S(1)} %get-tuple-element.41, f32[2048]{0:T(1024)S(1)} %get-tuple-element.40, bf16[1024,320]{1,0:T(8,128)(2,1)} %bitcast.92), kind=kOutput, calls=%fused_computation.19 | convolution fusion | flops 547880960 | bytes 9736192 | tf_op jit(solution)/shard_map/dot_general | solution.py:28
  110.0 1.4 reshape.244
  111.8 0.3 mul.110
  112.1 6.3 %convolution_convert_fusion = bf16[128,2560]{1,0:T(8,128)(2,1)S(1)} fusion(bf16[2048,2560]{1,0:T(8,128)(2,1)} %param.16, f32[128,2048]{1,0:T(8,128)S(1)} %reshape.244, f32[16,8,16,128]{3,2,1,0:T(8,128)S(1)} %bitcast.83, f32[128,2048]{1,0:T(8,128)S(1)} %reshape.242, f32[16,8,16,128]{3,2,1,0:T(8,128)S(1)} %bitcast.82), kind=kOutput, calls=%fused_computation.14 | convolution fusion | flops 1343553536 | bytes 15335424 | tf_op jit(solution)/shard_map/dot_general | solution.py:123
  118.4 1.1 copy.43
  119.5 26.1 %reduce-scatter.4.cloned.1.call-done = bf16[640,128]{1,0:T(8,128)(2,1)} async-done(((bf16[2560,128]{1,0:T(8,128)(2,1)}), bf16[640,128]{1,0:T(8,128)(2,1)}) %reduce-scatter.4.cloned.1.call-update) | async-done | bytes 163856
  145.6 1.7 %copy.44 = bf16[128,640]{1,0:T(8,128)(2,1)} copy(bf16[128,640]{0,1:T(8,128)(2,1)} %bitcast.93) | data formatting | bytes 327680
  (48 shorter events, 2.9 us)
Async XLA Ops:
  6.5 91.6 %copy-start = (bf16[128,2560]{1,0:T(8,128)(2,1)S(1)}, bf16[128,2560]{1,0:T(8,128)(2,1)}, u32[]{:S(2)}) copy-start(bf16[128,2560]{1,0:T(8,128)(2,1)} %param.14) | copy-start | bytes 1966084
  25.6 5.9 %copy-start.5 = (bf16[1,64,128]{2,1,0:T(8,128)(2,1)S(1)}, bf16[1,64,128]{2,1,0:T(8,128)(2,1)}, u32[]{:S(2)}) copy-start(bf16[1,64,128]{2,1,0:T(8,128)(2,1)} %param.13) | copy-start | bytes 49156
  25.8 52.7 %copy-start.4 = (bf16[1,64,192]{2,1,0:T(8,128)(2,1)S(1)}, bf16[1,64,192]{2,1,0:T(8,128)(2,1)}, u32[]{:S(2)}) copy-start(bf16[1,64,192]{2,1,0:T(8,128)(2,1)} %param.12) | copy-start | bytes 73732
  27.7 71.0 %all-to-all-start = ((bf16[8,4,64,320]{3,2,1,0:T(8,128)(2,1)}), bf16[8,4,64,320]{3,2,1,0:T(8,128)(2,1)S(1)}, u32[]{:S(2)}, u32[]{:S(2)}) async-start(bf16[8,4,64,320]{3,2,1,0:T(8,128)(2,1)} %maximum_select_fusion), calls=%async_computation | async-start | bytes 3145728 | tf_op jit(solution)/shard_map/all_to_all | solution.py:86
  31.3 114.3 %reduce-scatter.4.cloned.1.call-start = ((), (), s32[]{:S(2)}) async-start(), calls=%async_computation.2 | async-start | bytes 819200
  78.5 15.9 %copy-start.1 = (bf16[128,16,192]{2,1,0:T(8,128)(2,1)}, bf16[128,16,192]{2,1,0:T(8,128)(2,1)S(1)}, u32[]{:S(2)}) copy-start(bf16[128,16,192]{2,1,0:T(8,128)(2,1)S(1)} %copy.36) | copy-start | bytes 2359300
  93.7 0.9 copy-start.3
  94.6 3.5 %copy-start.2 = (bf16[1,2560,32]{1,2,0:T(8,128)(2,1)S(1)}, bf16[1,2560,32]{1,2,0:T(8,128)(2,1)}, u32[]{:S(2)}) copy-start(bf16[1,2560,32]{1,2,0:T(8,128)(2,1)} %param.15) | copy-start | bytes 491524
  94.6 4.0 %copy-start.6 = (s32[1,1,16]{2,1,0:T(1,128)S(1)}, s32[1,1,16]{2,1,0:T(1,128)}, u32[]{:S(2)}) copy-start(s32[1,1,16]{2,1,0:T(1,128)} %param.17) | copy-start | bytes 196
Sparse Core Ops, SparseCore 0:
  119.7 25.9 reduce-scatter.3
where the time goes:
time: 155 us; the launch traced here: 154 us
  blocking collectives  73.1 us (47%)
  waiting for transfers between devices  26.1 us (17%)
  matrix products  16.8 us (11%)
  local copies, waits for them, and re-layouts  14 us (9%)
  between operations  13.7 us (9%)
  other arithmetic  6.8 us (4%)
  starting transfers between devices  3.62 us (2%)
    all_gather x1, blocking collectives, shards(): piece_values = lax.all_gather(coarse_values[0], 'seq', axis=0, tiled=True)  45 us
    unnamed x2, waiting for transfers between devices  26.1 us
    all_gather x1, blocking collectives, shards(): piece_keys = lax.all_gather(coarse_keys[0], 'seq', axis=0, tiled=True)  14.4 us
    all_gather x1, blocking collectives, shards(): requests = lax.all_gather(selected[0], 'seq', axis=0, tiled=True)  13.7 us
    dot_general x2, matrix products, online_block(): jnp.dot(weights.astype(jnp.bfloat16), part_values, preferred_element_type...  6.69 us
    dot_general x1, matrix products, shards(): jnp.dot(attended, out_weight, preferred_element_type=jnp.float32)  6.32 us
    unnamed x18, local copies, waits for them, and re-layouts  6.06 us
    all_to_all x1, starting transfers between devices, shards(): lax.all_to_all(outgoing, 'seq', split_axis=0, concat_axis=0, tiled=True)  3.58 us
  transfers between devices with their start and end apart: 2, of which 1 were waited for; matrix products, arithmetic and copies ran while one was open for 5% of the time, Pallas kernels for 0%

commit v1 on v0

--- a/solution.py
+++ b/solution.py
@@ -59,7 +59,12 @@
         jnp.zeros((row_count,), jnp.float32),
         jnp.zeros((row_count, value_width), jnp.float32),
     )
-    requests = lax.all_gather(selected[0], "seq", axis=0, tiled=True)
+    ring = [selected[0]]
+    for hop in range(7):
+        ring.append(lax.ppermute(ring[-1], "seq", [(dev, (dev + 1) % 8) for dev in range(8)]))
+    requests = jnp.roll(
+        jnp.concatenate(ring[::-1], axis=0), (lax.axis_index("seq") + 1) * ring[0].shape[0], axis=0
+    )
     blocks_dev = ctx_dev // BLK
     slot_cap = max(1, 2 * SEL // seq_count)
     owners = requests // blocks_dev

time: 155 us -> 175 us (1.13)
  waiting for transfers between devices: 26.1 us -> 58.6 us
  blocking collectives: 73.1 us -> 59.5 us
    ppermute x0 -> x7, waiting for transfers between devices: none -> 32 us  [shards(): lax.ppermute(ring[-1], 'seq', [(dev, (dev + 1) % 8) for dev in range(8)])]
    all_gather x1 -> x0, blocking collectives: 13.7 us -> none  [shards(): requests = lax.all_gather(selected[0], 'seq', axis=0, tiled=True)]
  transfers between devices with their start and end apart: 2 -> 9, of which waited for: 1 -> 8; matrix products, arithmetic and copies ran while one was open for 5% -> 5% of each run, Pallas kernels for 0% -> 0%
where the time goes in v1:
time: 175 us
  blocking collectives  59.5 us (34%)
  waiting for transfers between devices  58.6 us (33%)
  matrix products  16.8 us (10%)
  local copies, waits for them, and re-layouts  15.4 us (9%)
  between operations  13.7 us (8%)
  other arithmetic  6.83 us (4%)
  starting transfers between devices  4.13 us (2%)
    all_gather x1, blocking collectives, shards(): piece_values = lax.all_gather(coarse_values[0], 'seq', axis=0, tiled=True)  45.1 us
    ppermute x7, waiting for transfers between devices, shards(): lax.ppermute(ring[-1], 'seq', [(dev, (dev + 1) % 8) for dev in range(8)])  32 us
    unnamed x2, waiting for transfers between devices  26.6 us
    all_gather x1, blocking collectives, shards(): piece_keys = lax.all_gather(coarse_keys[0], 'seq', axis=0, tiled=True)  14.4 us
    dot_general x2, matrix products, online_block(): jnp.dot(weights.astype(jnp.bfloat16), part_values, preferred_element_type...  6.68 us
    dot_general x1, matrix products, shards(): jnp.dot(attended, out_weight, preferred_element_type=jnp.float32)  6.33 us
    unnamed x18, local copies, waits for them, and re-layouts  6.06 us
    all_to_all x1, starting transfers between devices, shards(): lax.all_to_all(outgoing, 'seq', split_axis=0, concat_axis=0, tiled=True)  3.58 us
  transfers between devices with their start and end apart: 9, of which 8 were waited for; matrix products, arithmetic and copies ran while one was open for 5% of the time, Pallas kernels for 0%

profile of v1, /device:TPU:0, one launch (start us, length us, event | category | flops | bytes accessed | tf_op | source)
XLA Modules:
  0.0 174.9 jit_solution(14104723052976343747)
XLA Ops:
  8.0 4.5 %collective-permute-done = s32[1,16]{1,0:T(1,128)S(1)} collective-permute-done((s32[1,16]{1,0:T(1,128)}, s32[1,16]{1,0:T(1,128)S(1)}, u32[]{:S(2)}, u32[]{:S(2)}) %collective-permute-start) | collective-permute-done | bytes 96 | tf_op jit(solution)/shard_map/ppermute | solution.py:64
  12.4 4.8 %collective-permute-done.1 = s32[1,16]{1,0:T(1,128)S(1)} collective-permute-done((s32[1,16]{1,0:T(1,128)S(1)}, s32[1,16]{1,0:T(1,128)S(1)}, u32[]{:S(2)}, u32[]{:S(2)}) %collective-permute-start.1) | collective-permute-done | bytes 96 | tf_op jit(solution)/shard_map/ppermute | solution.py:64
  17.2 4.8 %collective-permute-done.2 = s32[1,16]{1,0:T(1,128)S(1)} collective-permute-done((s32[1,16]{1,0:T(1,128)S(1)}, s32[1,16]{1,0:T(1,128)S(1)}, u32[]{:S(2)}, u32[]{:S(2)}) %collective-permute-start.2) | collective-permute-done | bytes 96 | tf_op jit(solution)/shard_map/ppermute | solution.py:64
  22.0 4.8 %collective-permute-done.3 = s32[1,16]{1,0:T(1,128)S(1)} collective-permute-done((s32[1,16]{1,0:T(1,128)S(1)}, s32[1,16]{1,0:T(1,128)S(1)}, u32[]{:S(2)}, u32[]{:S(2)}) %collective-permute-start.3) | collective-permute-done | bytes 96 | tf_op jit(solution)/shard_map/ppermute | solution.py:64
  26.8 4.8 %collective-permute-done.4 = s32[1,16]{1,0:T(1,128)S(1)} collective-permute-done((s32[1,16]{1,0:T(1,128)S(1)}, s32[1,16]{1,0:T(1,128)S(1)}, u32[]{:S(2)}, u32[]{:S(2)}) %collective-permute-start.4) | collective-permute-done | bytes 96 | tf_op jit(solution)/shard_map/ppermute | solution.py:64
  32.8 3.6 %collective-permute-done.5 = s32[1,16]{1,0:T(1,128)S(1)} collective-permute-done((s32[1,16]{1,0:T(1,128)S(1)}, s32[1,16]{1,0:T(1,128)S(1)}, u32[]{:S(2)}, u32[]{:S(2)}) %collective-permute-start.5) | collective-permute-done | bytes 96 | tf_op jit(solution)/shard_map/ppermute | solution.py:64
  36.4 4.8 %collective-permute-done.6 = s32[1,16]{1,0:T(1,128)S(1)} collective-permute-done((s32[1,16]{1,0:T(1,128)S(1)}, s32[1,16]{1,0:T(1,128)S(1)}, u32[]{:S(2)}, u32[]{:S(2)}) %collective-permute-start.6) | collective-permute-done | bytes 96 | tf_op jit(solution)/shard_map/ppermute | solution.py:64
  41.2 1.4 concatenate.12
  44.0 1.6 gather_fusion.1
  46.0 1.9 %maximum_select_fusion = bf16[8,4,64,320]{3,2,1,0:T(8,128)(2,1)} fusion(bf16[8,4,64,128]{3,2,1,0:T(8,128)(2,1)S(1)} %broadcast_select_fusion.1, bf16[8,4,64,192]{3,2,1,0:T(8,128)(2,1)S(1)} %broadcast_select_fusion, pred[8,4]{1,0:T(8,128)(4,1)S(1)} %copy.36), kind=kLoop, calls=%fused_computation.20 | loop fusion | flops 3276800 | bytes 2621472 | tf_op jit(solution)/shard_map/jit(_where)/select_n | solution.py:90
  48.0 3.6 %all-to-all-start = ((bf16[8,4,64,320]{3,2,1,0:T(8,128)(2,1)}), bf16[8,4,64,320]{3,2,1,0:T(8,128)(2,1)S(1)}, u32[]{:S(2)}, u32[]{:S(2)}) async-start(bf16[8,4,64,320]{3,2,1,0:T(8,128)(2,1)} %maximum_select_fusion), calls=%async_computation | async-start | bytes 3145728 | tf_op jit(solution)/shard_map/all_to_all | solution.py:91
  51.6 45.1 %all-gather.1 = bf16[1,512,128]{2,1,0:T(8,128)(2,1)} all-gather(bf16[1,64,128]{2,1,0:T(8,128)(2,1)S(1)} %copy-done.5), channel_id=3, replica_groups=mesh['grp'=4,'seq'=8] {'seq'}, dimensions={1}, use_global_device_ids=true | all-gather | bytes 147456 | tf_op jit(solution)/shard_map/all_gather | solution.py:93
  97.0 1.8 %copy.34 = bf16[128,16,192]{2,1,0:T(8,128)(2,1)S(1)} copy(bf16[128,16,192]{0,2,1:T(8,128)(2,1)} %param.9) | data formatting | bytes 1572864 | tf_op args[0]
  98.8 14.4 %all-gather = bf16[1,512,192]{2,1,0:T(8,128)(2,1)S(1)} all-gather(bf16[1,64,192]{2,1,0:T(8,128)(2,1)S(1)} %copy-done.4), channel_id=2, replica_groups=mesh['grp'=4,'seq'=8] {'seq'}, dimensions={1}, use_global_device_ids=true | all-gather | bytes 221184 | tf_op jit(solution)/shard_map/all_gather | solution.py:92
  114.9 2.1 %fusion.8 = f32[2048,128]{1,0:T(8,128)} fusion(f32[2048,512]{0,1:T(8,128)S(1)} %get-tuple-element.49, f32[2048]{0:T(1024)S(1)} %broadcast_maximum_fusion.1, f32[2048]{0:T(1024)S(1)} %get-tuple-element.38, f32[2048]{0:T(1024)S(1)} %get-tuple-element.36, bf16[1,512,128]{2,1,0:T(8,128)(2,1)S(1)} %copy-done.3), kind=kOutput, calls=%fused_computation.16 | convolution fusion | flops 271056896 | bytes 5398528 | tf_op jit(solution)/shard_map/while/body/eval_jaxpr/dot_general | solution.py:28
  117.0 1.4 reshape.242
  118.9 1.5 gather_fusion.2
  120.5 2.7 %fusion.2 = (f32[2048]{0:T(1024)S(1)}, f32[1024,2048]{1,0:T(8,128)S(1)}) fusion(s32[2048]{0:T(1024)S(1)} %le.51, s32[1024]{0:T(1024)S(1)} %add.175, bf16[2048,192]{1,0:T(8,128)(2,1)} %bitcast.89, bf16[1024,320]{1,0:T(8,128)(2,1)} %bitcast.91), kind=kOutput, calls=%fused_computation.7 | convolution fusion | flops 813692928 | bytes 9981952 | tf_op jit(solution)/shard_map/dot_general | solution.py:18
  123.2 2.4 %fusion = f32[2048]{0:T(1024)S(1)} fusion(f32[1024,2048]{1,0:T(8,128)S(1)} %get-tuple-element.47, f32[2048]{0:T(1024)S(1)} %broadcast_maximum_fusion, s32[2048]{0:T(1024)S(1)} %le.51, s32[1024]{0:T(1024)S(1)} %add.175), kind=kLoop, calls=%fused_computation.5 | loop fusion | flops 10483712 | bytes 8417280 | tf_op jit(solution)/shard_map/reduce_sum | solution.py:27
  125.7 4.6 %fusion.14 = f32[2048,128]{1,0:T(8,128)} fusion(f32[1024,2048]{1,0:T(8,128)S(1)} %get-tuple-element.47, f32[2048]{0:T(1024)S(1)} %broadcast_maximum_fusion, s32[2048]{0:T(1024)S(1)} %le.51, s32[1024]{0:T(1024)S(1)} %add.175, f32[2048]{0:T(1024)S(1)} %get-tuple-element.41, f32[2048]{0:T(1024)S(1)} %get-tuple-element.40, bf16[1024,320]{1,0:T(8,128)(2,1)} %bitcast.92), kind=kOutput, calls=%fused_computation.19 | convolution fusion | flops 547880960 | bytes 9736192 | tf_op jit(solution)/shard_map/dot_general | solution.py:28
  130.3 1.4 reshape.244
  132.3 6.3 %convolution_convert_fusion = bf16[128,2560]{1,0:T(8,128)(2,1)S(1)} fusion(bf16[2048,2560]{1,0:T(8,128)(2,1)} %param.16, f32[128,2048]{1,0:T(8,128)S(1)} %reshape.244, f32[16,8,16,128]{3,2,1,0:T(8,128)S(1)} %bitcast.83, f32[128,2048]{1,0:T(8,128)S(1)} %reshape.242, f32[16,8,16,128]{3,2,1,0:T(8,128)S(1)} %bitcast.82), kind=kOutput, calls=%fused_computation.14 | convolution fusion | flops 1343553536 | bytes 15335424 | tf_op jit(solution)/shard_map/dot_general | solution.py:128
  139.8 26.6 %reduce-scatter.4.cloned.1.call-done = bf16[640,128]{1,0:T(8,128)(2,1)} async-done(((bf16[2560,128]{1,0:T(8,128)(2,1)}), bf16[640,128]{1,0:T(8,128)(2,1)}) %reduce-scatter.4.cloned.1.call-update) | async-done | bytes 163856
  166.3 1.7 copy.42
  (62 shorter events, 8.7 us)
Async XLA Ops:
  6.5 111.8 %copy-start = (bf16[128,2560]{1,0:T(8,128)(2,1)S(1)}, bf16[128,2560]{1,0:T(8,128)(2,1)}, u32[]{:S(2)}) copy-start(bf16[128,2560]{1,0:T(8,128)(2,1)} %param.14) | copy-start | bytes 1966084
  6.5 5.9 %collective-permute-start = (s32[1,16]{1,0:T(1,128)}, s32[1,16]{1,0:T(1,128)S(1)}, u32[]{:S(2)}, u32[]{:S(2)}) collective-permute-start(s32[1,16]{1,0:T(1,128)} %bitcast.94), channel_id=1, source_target_pairs={{0,1},{1,2},{2,3},{3,4},{4,5},{5,6},{6,7},{7,0},{8,9},{9,10},{10,1... | collective-permute-start | bytes 200 | tf_op jit(solution)/shard_map/ppermute | solution.py:64
  12.4 4.8 %collective-permute-start.1 = (s32[1,16]{1,0:T(1,128)S(1)}, s32[1,16]{1,0:T(1,128)S(1)}, u32[]{:S(2)}, u32[]{:S(2)}) collective-permute-start(s32[1,16]{1,0:T(1,128)S(1)} %collective-permute-done), channel_id=1, source_target_pairs={{0,1},{1,2},{2,3},{3,4},{4,5},{5,6},{6,7},{7,0},{8,9},{9,10},{10,1... | collective-permute-start | bytes 200 | tf_op jit(solution)/shard_map/ppermute | solution.py:64
  17.2 4.8 %collective-permute-start.2 = (s32[1,16]{1,0:T(1,128)S(1)}, s32[1,16]{1,0:T(1,128)S(1)}, u32[]{:S(2)}, u32[]{:S(2)}) collective-permute-start(s32[1,16]{1,0:T(1,128)S(1)} %collective-permute-done.1), channel_id=1, source_target_pairs={{0,1},{1,2},{2,3},{3,4},{4,5},{5,6},{6,7},{7,0},{8,9},{9,10},{10,1... | collective-permute-start | bytes 200 | tf_op jit(solution)/shard_map/ppermute | solution.py:64
  22.0 4.8 %collective-permute-start.3 = (s32[1,16]{1,0:T(1,128)S(1)}, s32[1,16]{1,0:T(1,128)S(1)}, u32[]{:S(2)}, u32[]{:S(2)}) collective-permute-start(s32[1,16]{1,0:T(1,128)S(1)} %collective-permute-done.2), channel_id=1, source_target_pairs={{0,1},{1,2},{2,3},{3,4},{4,5},{5,6},{6,7},{7,0},{8,9},{9,10},{10,1... | collective-permute-start | bytes 200 | tf_op jit(solution)/shard_map/ppermute | solution.py:64
  26.8 4.8 %collective-permute-start.4 = (s32[1,16]{1,0:T(1,128)S(1)}, s32[1,16]{1,0:T(1,128)S(1)}, u32[]{:S(2)}, u32[]{:S(2)}) collective-permute-start(s32[1,16]{1,0:T(1,128)S(1)} %collective-permute-done.3), channel_id=1, source_target_pairs={{0,1},{1,2},{2,3},{3,4},{4,5},{5,6},{6,7},{7,0},{8,9},{9,10},{10,1... | collective-permute-start | bytes 200 | tf_op jit(solution)/shard_map/ppermute | solution.py:64
  31.6 4.8 %collective-permute-start.5 = (s32[1,16]{1,0:T(1,128)S(1)}, s32[1,16]{1,0:T(1,128)S(1)}, u32[]{:S(2)}, u32[]{:S(2)}) collective-permute-start(s32[1,16]{1,0:T(1,128)S(1)} %collective-permute-done.4), channel_id=1, source_target_pairs={{0,1},{1,2},{2,3},{3,4},{4,5},{5,6},{6,7},{7,0},{8,9},{9,10},{10,1... | collective-permute-start | bytes 200 | tf_op jit(solution)/shard_map/ppermute | solution.py:64
  36.4 4.8 %collective-permute-start.6 = (s32[1,16]{1,0:T(1,128)S(1)}, s32[1,16]{1,0:T(1,128)S(1)}, u32[]{:S(2)}, u32[]{:S(2)}) collective-permute-start(s32[1,16]{1,0:T(1,128)S(1)} %collective-permute-done.5), channel_id=1, source_target_pairs={{0,1},{1,2},{2,3},{3,4},{4,5},{5,6},{6,7},{7,0},{8,9},{9,10},{10,1... | collective-permute-start | bytes 200 | tf_op jit(solution)/shard_map/ppermute | solution.py:64
  45.8 5.8 %copy-start.5 = (bf16[1,64,128]{2,1,0:T(8,128)(2,1)S(1)}, bf16[1,64,128]{2,1,0:T(8,128)(2,1)}, u32[]{:S(2)}) copy-start(bf16[1,64,128]{2,1,0:T(8,128)(2,1)} %param.13) | copy-start | bytes 49156
  46.0 52.7 %copy-start.4 = (bf16[1,64,192]{2,1,0:T(8,128)(2,1)S(1)}, bf16[1,64,192]{2,1,0:T(8,128)(2,1)}, u32[]{:S(2)}) copy-start(bf16[1,64,192]{2,1,0:T(8,128)(2,1)} %param.12) | copy-start | bytes 73732
  48.0 71.0 %all-to-all-start = ((bf16[8,4,64,320]{3,2,1,0:T(8,128)(2,1)}), bf16[8,4,64,320]{3,2,1,0:T(8,128)(2,1)S(1)}, u32[]{:S(2)}, u32[]{:S(2)}) async-start(bf16[8,4,64,320]{3,2,1,0:T(8,128)(2,1)} %maximum_select_fusion), calls=%async_computation | async-start | bytes 3145728 | tf_op jit(solution)/shard_map/all_to_all | solution.py:91
  51.6 114.8 %reduce-scatter.4.cloned.1.call-start = ((), (), s32[]{:S(2)}) async-start(), calls=%async_computation.2 | async-start | bytes 819200
  98.8 15.9 %copy-start.1 = (bf16[128,16,192]{2,1,0:T(8,128)(2,1)}, bf16[128,16,192]{2,1,0:T(8,128)(2,1)S(1)}, u32[]{:S(2)}) copy-start(bf16[128,16,192]{2,1,0:T(8,128)(2,1)S(1)} %copy.34) | copy-start | bytes 2359300
  114.0 0.9 copy-start.3
  114.9 3.5 %copy-start.2 = (bf16[1,2560,32]{1,2,0:T(8,128)(2,1)S(1)}, bf16[1,2560,32]{1,2,0:T(8,128)(2,1)}, u32[]{:S(2)}) copy-start(bf16[1,2560,32]{1,2,0:T(8,128)(2,1)} %param.15) | copy-start | bytes 491524
  114.9 4.0 %copy-start.6 = (s32[1,1,16]{2,1,0:T(1,128)S(1)}, s32[1,1,16]{2,1,0:T(1,128)}, u32[]{:S(2)}) copy-start(s32[1,1,16]{2,1,0:T(1,128)} %param.17) | copy-start | bytes 196
Sparse Core Ops, SparseCore 0:
  139.9 26.4 reduce-scatter.3
